TPU v7x, 1024 devices: a whole 4x8x16 slice. The times are simulated.
1024 devices in a mesh: dp: 64 (over z_lo, y, core), vox: 16 (over z_hi, x).
Axes of the slice: x: 4, y: 8, z: 16 (z_hi: 4, z_lo: 4; z = z_hi * 4 + z_lo), core: 2. Of those that a mesh axis runs over, the one named last changes fastest.
Arguments:
- kernels: bfloat16 [3072, 65536], P('dp', 'vox'), may hold values from -0.0234375 to 0.0234375
- observed: float32 [8, 3072], P(None, 'dp'), may hold values from -6 to 6
- initial: float32 [8, 65536], P(None, 'vox'), may hold values from -6 to 6
- threshold: float32 [8, 16, 2], replicated, may hold values from 0.05 to 0.5
Outputs:
- coefficients: float32 [8, 65536], P(None, 'vox')
- residual: float32 [8, 3072], P(None, 'dp')
All inputs are finite; a program needn't handle non-finite values.
Results may differ from a plain program's by a relative error of at most 0.0043.
Values may be sent and summed in bfloat16 or wider, within the bound.
A program may use at most 32 MiB of HBM per device.

v0:
```python
import jax
import jax.numpy as jnp
from jax import lax
from jax.sharding import PartitionSpec as P

ITERS = 2


step_size = 0.5


def passed_along(block, axis, distance):
    devices = range(lax.axis_size(axis))
    route = [((i - distance) % len(devices), i) for i in devices]
    return lax.ppermute(block, axis, route)


def from_right(edge):
    return passed_along(edge, "vox", -1)


def from_left(edge):
    return passed_along(edge, "vox", 1)


def forward_wave(arranged):
    even_part = arranged[..., 0, :]
    odd_part = arranged[..., 1, :]
    even_next = jnp.concatenate([even_part[..., 1:], from_right(even_part[..., :1])], axis=-1)
    detail = odd_part - 0.5 * (even_part + even_next)
    detail_prev = jnp.concatenate([from_left(detail[..., -1:]), detail[..., :-1]], axis=-1)
    smooth = even_part + 0.25 * (detail_prev + detail)
    return jnp.stack([smooth, detail], axis=-2)


def inverse_wave(arranged):
    smooth = arranged[..., 0, :]
    detail = arranged[..., 1, :]
    detail_prev = jnp.concatenate([from_left(detail[..., -1:]), detail[..., :-1]], axis=-1)
    even_part = smooth - 0.25 * (detail_prev + detail)
    even_next = jnp.concatenate([even_part[..., 1:], from_right(even_part[..., :1])], axis=-1)
    odd_part = detail + 0.5 * (even_part + even_next)
    return jnp.stack([even_part, odd_part], axis=-2)


def shrink(values, thresholds):
    return jnp.sign(values) * jnp.maximum(jnp.abs(values) - thresholds, 0.0)


def body(kernels, observed, initial, threshold):
    models_count = initial.shape[0]
    block_width = initial.shape[1]
    layer_count = threshold.shape[1]
    half_cells = block_width // (2 * layer_count)
    wavelets = initial.reshape(models_count, layer_count, 2, half_cells)
    voxel_model = inverse_wave(wavelets).reshape(models_count, block_width).astype(jnp.bfloat16)
    cutoff = threshold[..., None]
    residual = observed
    for iteration in range(ITERS):
        partial_pred = lax.dot_general(
            voxel_model, kernels, (((1,), (1,)), ((), ())), preferred_element_type=jnp.float32
        )
        predicted = lax.psum(partial_pred, "vox")
        residual = observed - predicted
        partial_grad = jnp.dot(
            residual.astype(jnp.bfloat16), kernels, preferred_element_type=jnp.float32
        )
        final_turn = iteration + 1 == ITERS
        gradient = lax.psum(partial_grad, "dp").reshape(models_count, layer_count, 2, half_cells)
        wavelets = shrink(wavelets + step_size * forward_wave(gradient), cutoff)
        if not final_turn:
            voxel_model = (
                inverse_wave(wavelets).reshape(models_count, block_width).astype(jnp.bfloat16)
            )
    coefficients = wavelets.reshape(models_count, block_width)
    return (coefficients, residual)


def solution(mesh):
    return jax.shard_map(
        body,
        mesh=mesh,
        in_specs=(P("dp", "vox"), P(None, "dp"), P(None, "vox"), P()),
        out_specs=(P(None, "vox"), P(None, "dp")),
        check_vma=False,
    )
```

profile of v0, /device:TPU:1, one launch (start us, length us, event | category | flops | bytes accessed | tf_op | source)
XLA Modules:
  0.0 1189.0 jit_solution(12076960843054306961)
XLA Ops:
  7.2 1.1 reshape.51
  8.3 0.1 fusion.35
  8.4 0.1 slice.98
  8.5 3.9 collective-permute-start
  12.5 18.8 %collective-permute-done = f32[8,16,1]{2,1,0:T(8,128)S(1)} collective-permute-done((f32[8,16,1]{2,1,0:T(8,128)S(1)}, f32[8,16,1]{2,1,0:T(8,128)S(1)}, u32[]{:S(2)}, u32[]{:S(2)}) %collective-permute-start) | collective-permute-done | bytes 544 | tf_op jit(solution)/shard_map/ppermute | solution.py:15
  31.3 0.1 fusion.6
  31.4 3.1 collective-permute-start.1
  34.5 0.1 slice_bitcast_fusion.3
  34.6 1.8 collective-permute-done.1
  36.4 0.1 fusion.30
  36.5 0.1 copy.99
  36.7 0.2 fusion.37
  36.9 46.5 %psum.28 = f32[8,48]{1,0:T(8,128)S(1)} all-reduce(f32[8,48]{1,0:T(8,128)S(1)} %fusion.37), channel_id=1, replica_groups=mesh['dp'=64,'vox'=16] {'vox'}, use_global_device_ids=true, to_apply=%region_0.0 | all-reduce | flops 384 | bytes 3072 | tf_op jit(solution)/shard_map/psum | solution.py:63
  83.4 0.2 fusion.27
  83.6 0.1 reshape.52
  83.7 0.7 copy.100
  84.4 0.0 all-reduce.5.cloned.1.call-start
  84.5 496.9 %all-reduce.3.cloned.1.call-done = f32[8,16,2,128]{3,1,0,2:T(8,128)} async-done(((f32[8,16,2,128]{3,1,0,2:T(8,128)}), f32[8,16,2,128]{3,1,0,2:T(8,128)}) %all-reduce.3.cloned.1.call-update) | async-done | bytes 131088 | tf_op jit(solution)/shard_map/psum | solution.py:69
  581.4 0.8 slice_bitcast_fusion.6
  582.2 9.0 collective-permute-start.2
  591.2 0.1 slice_bitcast_fusion.9
  591.3 1.2 collective-permute-done.2
  592.5 0.1 fusion.8
  592.6 0.1 slice.106
  592.7 1.9 collective-permute-start.3
  594.7 9.6 collective-permute-done.3
  604.2 0.1 fusion.10
  604.3 0.6 copy-done.4
  604.9 0.1 copy_multiply_fusion
  605.0 0.1 slice.110
  605.1 1.9 collective-permute-start.4
  607.1 9.1 collective-permute-done.4
  616.2 0.1 fusion.15
  616.3 1.9 collective-permute-start.5
  618.2 0.1 fusion.32
  618.3 0.1 slice_bitcast_fusion.1
  618.4 2.9 collective-permute-done.5
  621.3 0.1 fusion.18
  621.4 0.1 copy.114
  621.5 0.2 fusion.38
  621.7 45.3 %psum.30 = f32[8,48]{1,0:T(8,128)S(1)} all-reduce(f32[8,48]{1,0:T(8,128)S(1)} %fusion.38), channel_id=1, replica_groups=mesh['dp'=64,'vox'=16] {'vox'}, use_global_device_ids=true, to_apply=%region_2.0 | all-reduce | flops 384 | bytes 3072 | tf_op jit(solution)/shard_map/psum | solution.py:63
  667.0 0.2 fusion.28
  667.2 0.4 copy-done.6
  667.6 0.1 reshape.53
  667.8 0.7 copy.115
  668.4 0.1 copy.126
  668.6 0.2 sub.59.clone
  668.8 0.1 sub.60
  668.9 0.1 copy.105
  669.0 0.1 mul.75
  669.1 488.5 %all-reduce.5.cloned.1.call-done = f32[8,16,2,128]{3,1,0,2:T(8,128)} async-done(((f32[8,16,2,128]{3,1,0,2:T(8,128)}), f32[8,16,2,128]{3,1,0,2:T(8,128)}) %all-reduce.5.cloned.1.call-update) | async-done | bytes 131088 | tf_op jit(solution)/shard_map/psum | solution.py:69
  1157.6 0.8 slice_bitcast_fusion.4
  1158.4 9.0 collective-permute-start.6
  1167.4 0.1 slice_bitcast_fusion.7
  1167.5 1.2 collective-permute-done.6
  1168.7 0.1 fusion.20
  1168.8 0.1 slice.118
  1168.9 1.9 collective-permute-start.7
  1170.8 9.4 collective-permute-done.7
  1180.2 0.1 fusion.23
  1180.4 0.1 copy.122
  1180.5 0.1 mul.85
  1180.6 0.8 copy-done.3
  1181.4 0.8 maximum_multiply_fusion.1
  (25 shorter events, 0.2 us)
Async XLA Ops:
  7.2 29.5 %copy-start = (bf16[48,4096]{1,0:T(8,128)(2,1)S(1)}, bf16[48,4096]{1,0:T(8,128)(2,1)}, u32[]{:S(2)}) copy-start(bf16[48,4096]{1,0:T(8,128)(2,1)} %param.4) | copy-start | bytes 1179652
  7.2 574.2 %all-reduce.3.cloned.1.call-start = ((), (), s32[]{:S(2)}) async-start(), calls=%async_computation | async-start | bytes 262144 | tf_op jit(solution)/shard_map/psum | solution.py:69
  8.5 22.8 %collective-permute-start = (f32[8,16,1]{2,1,0:T(8,128)S(1)}, f32[8,16,1]{2,1,0:T(8,128)S(1)}, u32[]{:S(2)}, u32[]{:S(2)}) collective-permute-start(f32[8,16,1]{2,1,0:T(8,128)S(1)} %slice.98), channel_id=1, source_target_pairs={{15,0},{0,1},{1,2},{2,3},{3,4},{4,5},{5,6},{6,7},{7,8},{8,9},{9,10... | collective-permute-start | bytes 1544 | tf_op jit(solution)/shard_map/ppermute | solution.py:15
  31.4 5.0 collective-permute-start.1
  36.9 46.6 %copy-start.5 = (f32[8,48]{1,0:T(8,128)S(1)}, f32[8,48]{1,0:T(8,128)}, u32[]{:S(2)}) copy-start(f32[8,48]{1,0:T(8,128)} %param.5) | copy-start | bytes 4612
  84.4 1073.2 %all-reduce.5.cloned.1.call-start = ((), (), s32[]{:S(2)}) async-start(), calls=%async_computation.1 | async-start | bytes 262144 | tf_op jit(solution)/shard_map/psum | solution.py:69
  582.2 10.3 copy-start.2
  582.2 10.3 collective-permute-start.2
  592.7 11.5 collective-permute-start.3
  604.2 0.7 copy-start.4
  605.1 11.1 collective-permute-start.4
  616.3 5.0 collective-permute-start.5
  667.0 0.6 copy-start.6
  1158.4 10.3 copy-start.1
  1158.4 10.3 collective-permute-start.6
  1168.9 11.4 collective-permute-start.7
  1180.4 0.9 copy-start.3
Sparse Core Ops, SparseCore 0:
  84.5 496.8 all-reduce.2
  668.6 488.9 all-reduce.4
where the time goes:
time: 1190 us
  waiting for transfers between devices  1040 us (87%)
  blocking collectives  91.9 us (8%)
  starting transfers between devices  32.8 us (3%)
  between operations  14.4 us (1%)
    psum x2, waiting for transfers between devices, body(): lax.psum(partial_grad, 'dp')  985 us
    psum x2, blocking collectives, body(): predicted = lax.psum(partial_pred, 'vox')  91.9 us
    ppermute x8, waiting for transfers between devices, passed_along(): return lax.ppermute(block, axis, route)  54.1 us
    ppermute x8, starting transfers between devices, passed_along(): return lax.ppermute(block, axis, route)  32.7 us
  transfers between devices with their start and end apart: 10, of which 10 were waited for; matrix products, arithmetic and copies ran while one was open for 0% of the time, Pallas kernels for 0%

commit v1 on v0

v1 whole, which is shorter than its diff:
```python
import functools

import jax
import jax.numpy as jnp
from jax import lax
from jax.experimental import pallas as pl
from jax.experimental.pallas import tpu as pltpu
from jax.sharding import PartitionSpec as P

MESH = pl.DeviceIdType.MESH
F32 = jnp.float32
BF16 = jnp.bfloat16
LANES = 128
LAYERS = 16
SLOTS = 8

NC, NY, NZ, NV = 2, 8, 4, 16


def lane_of(rows=8):
    return lax.broadcasted_iota(jnp.int32, (rows, LANES), 1)


def shrink(values, cutoff):
    return jnp.where(
        values > cutoff, values - cutoff, jnp.where(values < -cutoff, values + cutoff, 0.0)
    )


def take_prev(tile, edge):
    return jnp.where(lane_of() == 0, edge, pltpu.roll(tile, 1, 1))


def take_next(tile, edge):
    return jnp.where(lane_of() == LANES - 1, edge, pltpu.roll(tile, LANES - 1, 1))


def inverse_wave(smooth, detail, detail_before, smooth_after, detail_after):
    even = smooth - 0.25 * (take_prev(detail, detail_before) + detail)
    even_after = smooth_after - 0.25 * (detail[:, LANES - 1 :] + detail_after)
    odd = detail + 0.5 * (even + take_next(even, even_after))
    return even, odd


def rows_dot(a, b):
    return lax.dot_general(a, b, (((1,), (1,)), ((), ())), preferred_element_type=F32)


def kernel(
    sizes,
    k_ref,
    obs_ref,
    init_ref,
    thr_ref,
    coef_ref,
    resid_ref,
    pack,
    packs,
    edge_f32,
    edge,
    edges,
    model,
    pred_pad,
    pred_send,
    preds,
    stage,
    parts,
    sums_send,
    sums,
    chunks,
    finals,
    send_sem,
    recv_sem,
):
    nc, ny, nz, nv = sizes
    groups = nc * nz
    per = LAYERS // groups
    width = per * 2 * LANES
    rows = k_ref.shape[0]
    dp = lax.axis_index("dp")
    vox = lax.axis_index("vox")
    core = lax.rem(dp, nc)
    y = lax.rem(lax.div(dp, nc), ny)
    z = lax.div(dp, nc * ny)
    g = z * nc + core

    def vox_peer(k):
        return dp, lax.rem(vox + k, nv)

    def group_peer(k):
        other = lax.rem(g + k, groups)
        return (lax.div(other, nc) * ny + y) * nc + lax.rem(other, nc), vox

    def y_peer(k):
        return (z * ny + lax.rem(y + k, ny)) * nc + core, vox

    barrier = pltpu.get_barrier_semaphore()

    def greet(peer, count):
        def one(k, carry):
            pl.semaphore_signal(barrier, inc=1, device_id=peer(k), device_id_type=MESH)
            return carry

        lax.fori_loop(1, count, one, 0)

    greet(vox_peer, nv)
    greet(group_peer, groups)
    greet(y_peer, ny)

    def send(src, dst, phase, device):
        pltpu.make_async_remote_copy(
            src_ref=src,
            dst_ref=dst,
            send_sem=send_sem.at[phase],
            recv_sem=recv_sem.at[phase],
            device_id=device,
            device_id_type=MESH,
        ).start()

    def wait(ref, sem, phase):
        pltpu.make_async_copy(ref, ref, sem.at[phase]).wait()

    lane = lane_of()
    packed = jnp.zeros((8, LANES), F32)
    for layer in range(LAYERS):
        base = layer * 2 * LANES
        smooth = init_ref[:, base : base + LANES]
        detail = init_ref[:, base + LANES : base + 2 * LANES]
        at = layer * SLOTS
        if at:
            packed = jnp.where(lane == at, pltpu.roll(smooth, at, 1), packed)
        else:
            packed = jnp.where(lane == at, smooth, packed)
        packed = jnp.where(lane == at + 1, pltpu.roll(detail, at + 1, 1), packed)
        packed = jnp.where(lane == at + 4, pltpu.roll(detail, at + 5, 1), packed)
    pack[...] = packed
    slot = lax.broadcasted_iota(jnp.int32, (SLOTS, 2 * LANES), 0)
    column = lax.broadcasted_iota(jnp.int32, (SLOTS, 2 * LANES), 1)
    picked = (
        ((slot == 0) & (column == 0))
        | ((slot == 1) & (column == LANES))
        | ((slot == 2) & (column == 1))
        | ((slot == 3) & (column == LANES - 1))
        | ((slot == 4) & (column == 2 * LANES - 1))
    )
    pick = jnp.where(picked, 1.0, 0.0).astype(BF16)
    edge_f32[...] = jnp.zeros_like(edge_f32)
    pred_pad[...] = jnp.zeros_like(pred_pad)
    for layer in range(LAYERS):
        base = layer * 2 * LANES
        edge_f32[layer * SLOTS : (layer + 1) * SLOTS, 0:rows] = rows_dot(
            pick, k_ref[:, base : base + 2 * LANES]
        )
    edge[...] = edge_f32[...].astype(BF16)

    pl.semaphore_wait(barrier, (nv - 1) + (groups - 1) + (ny - 1))

    send(pack, packs.at[0], 0, vox_peer(nv - 1))
    send(pack, packs.at[1], 0, vox_peer(1))
    send(edge, edges.at[0], 1, vox_peer(nv - 1))
    send(edge, edges.at[1], 1, vox_peer(1))

    wait(packs, recv_sem, 0)
    after = packs[0]
    before = packs[1]
    for layer in range(LAYERS):
        base = layer * 2 * LANES
        at = layer * SLOTS
        even, odd = inverse_wave(
            init_ref[:, base : base + LANES],
            init_ref[:, base + LANES : base + 2 * LANES],
            before[:, at + 4 : at + 5],
            after[:, at : at + 1],
            after[:, at + 1 : at + 2],
        )
        model[:, base : base + LANES] = even.astype(BF16)
        model[:, base + LANES : base + 2 * LANES] = odd.astype(BF16)
    pred = rows_dot(model[...], k_ref[...])

    mine = pl.ds(pl.multiple_of(g * width, width), width)
    back = lax.rem(LANES - g * (per * SLOTS), LANES)
    after = pltpu.roll(after, back, 1)
    before = pltpu.roll(before, back, 1)
    pred_pad[:, 64:80] = thr_ref[:, 0, :]
    pred_pad[:, 96:112] = thr_ref[:, 1, :]
    cutoffs = pltpu.roll(pred_pad[...], lax.rem(LANES - g * per, LANES), 1)
    own = init_ref[:, mine]
    state = []
    for i in range(per):
        base = i * 2 * LANES
        at = i * SLOTS
        state.append(
            (
                own[:, base : base + LANES],
                own[:, base + LANES : base + 2 * LANES],
                before[:, at + 4 : at + 5],
                after[:, at : at + 1],
                after[:, at + 1 : at + 2],
            )
        )

    for it in range(2):
        phase = 2 + 4 * it
        pred_pad[:, 0:rows] = pred
        padded = jnp.where(lane < rows, pred_pad[...], 0.0)
        shared = padded[0:4] + pltpu.roll(padded[4:8], rows, 1)
        pred_send[it] = shared
        preds[it, vox] = shared

        def send_pred(k, carry):
            send(pred_send.at[it], preds.at[it, vox], phase, vox_peer(k))
            return carry

        lax.fori_loop(1, nv, send_pred, 0)
        wait(preds.at[it, pl.ds(0, nv - 1)], recv_sem, phase)
        total = preds[it, 0]
        for j in range(1, nv):
            total = total + preds[it, j]
        predicted = jnp.concatenate(
            [total[:, 0:rows], pltpu.roll(total, LANES - rows, 1)[:, 0:rows]], axis=0
        )
        residual = obs_ref[...] - predicted
        sent = residual.astype(BF16)

        if it == 0:
            wait(edges, recv_sem, 1)
            place = lax.rem(
                lax.broadcasted_iota(jnp.int32, (LAYERS * SLOTS, LANES), 0), SLOTS
            )
            edge_f32[...] = jnp.where(
                place < 3, edges[0].astype(F32), edges[1].astype(F32)
            )
        else:
            resid_ref[...] = residual
        grad = jnp.dot(sent, k_ref[...], preferred_element_type=F32).astype(BF16)
        edge_grad = rows_dot(sent, edge_f32[:, 0:rows].astype(BF16)).astype(BF16)
        for i in range(groups):
            stage[it, i, :, 0:width] = grad[:, i * width : (i + 1) * width]
            stage[it, i, :, width:] = edge_grad

        def send_part(k, carry):
            other = lax.rem(g + k, groups)
            send(stage.at[it, other], parts.at[it, k - 1], phase + 1, group_peer(k))
            return carry

        lax.fori_loop(1, groups, send_part, 0)
        wait(parts.at[it], recv_sem, phase + 1)
        total = stage[it, g].astype(F32)
        for i in range(groups - 1):
            total = total + parts[it, i].astype(F32)
        total = total.astype(BF16)
        sums_send[it] = total
        sums[it, y] = total

        def send_sum(k, carry):
            send(sums_send.at[it], sums.at[it, y], phase + 2, y_peer(k))
            return carry

        lax.fori_loop(1, ny, send_sum, 0)
        wait(sums.at[it, pl.ds(0, ny - 1)], recv_sem, phase + 2)
        total = sums[it, 0].astype(F32)
        for i in range(1, ny):
            total = total + sums[it, i].astype(F32)
        beside = pltpu.roll(total[:, width:], back, 1)

        for i in range(per):
            base = i * 2 * LANES
            at = i * SLOTS
            even = total[:, base : base + LANES]
            odd = total[:, base + LANES : base + 2 * LANES]
            even_after = beside[:, at : at + 1]
            odd_after = beside[:, at + 1 : at + 2]
            even_after2 = beside[:, at + 2 : at + 3]
            even_before = beside[:, at + 3 : at + 4]
            odd_before = beside[:, at + 4 : at + 5]
            detail = odd - 0.5 * (even + take_next(even, even_after))
            detail_before = odd_before - 0.5 * (even_before + even[:, 0:1])
            smooth = even + 0.25 * (take_prev(detail, detail_before) + detail)
            cut_s = cutoffs[:, 64 + i : 65 + i]
            cut_d = cutoffs[:, 96 + i : 97 + i]
            w_s, w_d, w_db, w_sa, w_da = state[i]
            w_s = shrink(w_s + 0.5 * smooth, cut_s)
            w_d = shrink(w_d + 0.5 * detail, cut_d)
            if it == 0:
                detail_after = odd_after - 0.5 * (even_after + even_after2)
                smooth_after = even_after + 0.25 * (detail[:, LANES - 1 :] + detail_after)
                w_db = shrink(w_db + 0.5 * detail_before, cut_d)
                w_sa = shrink(w_sa + 0.5 * smooth_after, cut_s)
                w_da = shrink(w_da + 0.5 * detail_after, cut_d)
                state[i] = (w_s, w_d, w_db, w_sa, w_da)
                even, odd = inverse_wave(w_s, w_d, w_db, w_sa, w_da)
                chunks[g, :, base : base + LANES] = even.astype(BF16)
                chunks[g, :, base + LANES : base + 2 * LANES] = odd.astype(BF16)
            else:
                finals[g, :, base : base + LANES] = w_s
                finals[g, :, base + LANES : base + 2 * LANES] = w_d

        target = chunks if it == 0 else finals

        def send_chunk(k, carry):
            send(target.at[g], target.at[g], phase + 3, group_peer(k))
            return carry

        lax.fori_loop(1, groups, send_chunk, 0)
        wait(target.at[pl.ds(0, groups - 1)], recv_sem, phase + 3)
        if it == 0:
            pred = rows_dot(chunks[0], k_ref[:, 0:width])
            for i in range(1, groups):
                pred = pred + rows_dot(chunks[i], k_ref[:, i * width : (i + 1) * width])
        else:
            for i in range(groups):
                coef_ref[:, i * width : (i + 1) * width] = finals[i]

    wait(packs, send_sem, 0)
    wait(edges, send_sem, 1)
    for it in range(2):
        phase = 2 + 4 * it
        target = chunks if it == 0 else finals
        wait(preds.at[it, pl.ds(0, nv - 1)], send_sem, phase)
        wait(parts.at[it], send_sem, phase + 1)
        wait(sums.at[it, pl.ds(0, ny - 1)], send_sem, phase + 2)
        wait(target.at[pl.ds(0, groups - 1)], send_sem, phase + 3)


def body(sizes, kernels, observed, initial, threshold):
    nc, ny, nz, nv = sizes
    groups = nc * nz
    width = (LAYERS // groups) * 2 * LANES
    vmem = pl.BlockSpec(memory_space=pltpu.VMEM)
    wide = width + LANES
    return pl.pallas_call(
        functools.partial(kernel, sizes),
        out_shape=(
            jax.ShapeDtypeStruct(initial.shape, F32),
            jax.ShapeDtypeStruct(observed.shape, F32),
        ),
        in_specs=[vmem] * 4,
        out_specs=(vmem, vmem),
        scratch_shapes=[
            pltpu.VMEM((8, LANES), F32),
            pltpu.VMEM((2, 8, LANES), F32),
            pltpu.VMEM((LAYERS * SLOTS, LANES), F32),
            pltpu.VMEM((LAYERS * SLOTS, LANES), BF16),
            pltpu.VMEM((2, LAYERS * SLOTS, LANES), BF16),
            pltpu.VMEM(initial.shape, BF16),
            pltpu.VMEM((8, LANES), F32),
            pltpu.VMEM((2, 4, LANES), F32),
            pltpu.VMEM((2, nv, 4, LANES), F32),
            pltpu.VMEM((2, groups, 8, wide), BF16),
            pltpu.VMEM((2, groups - 1, 8, wide), BF16),
            pltpu.VMEM((2, 8, wide), BF16),
            pltpu.VMEM((2, ny, 8, wide), BF16),
            pltpu.VMEM((groups, 8, width), BF16),
            pltpu.VMEM((groups, 8, width), F32),
            pltpu.SemaphoreType.DMA((10,)),
            pltpu.SemaphoreType.DMA((10,)),
        ],
        compiler_params=pltpu.CompilerParams(collective_id=0, has_side_effects=True),
    )(kernels, observed, initial, jnp.transpose(threshold, (0, 2, 1)))


def build(mesh, sizes):
    return jax.shard_map(
        functools.partial(body, sizes),
        mesh=mesh,
        in_specs=(P("dp", "vox"), P(None, "dp"), P(None, "vox"), P()),
        out_specs=(P(None, "vox"), P(None, "dp")),
        check_vma=False,
    )


def solution(mesh):
    return build(mesh, (NC, NY, NZ, NV))
```

time: 1190 us -> 79.3 us (0.07)
  waiting for transfers between devices: 1040 us -> 0 us
  blocking collectives: 91.9 us -> 0 us
  Pallas kernels: 0 us -> 76.3 us
  starting transfers between devices: 32.8 us -> 0 us
  between operations: 14.4 us -> 0.65 us
    psum x2 -> x0, waiting for transfers between devices: 985 us -> none  [body(): lax.psum(partial_grad, 'dp')]
    psum x2 -> x0, blocking collectives: 91.9 us -> none  [body(): predicted = lax.psum(partial_pred, 'vox')]
    pallas_call x0 -> x1, Pallas kernels: none -> 76.3 us  [body(): pl.pallas_call(functools.partial(kernel, sizes), out_shape=(jax.ShapeDtyp...]
    ppermute x8 -> x0, waiting for transfers between devices: 54.1 us -> none  [passed_along(): return lax.ppermute(block, axis, route)]
    ppermute x8 -> x0, starting transfers between devices: 32.7 us -> none  [passed_along(): return lax.ppermute(block, axis, route)]
  transfers between devices with their start and end apart: 10 -> 0, of which waited for: 10 -> 0; matrix products, arithmetic and copies ran while one was open for 0% -> 0% of each run, Pallas kernels for 0% -> 0%
where the time goes in v1:
time: 79.3 us; the launch traced here: 79.1 us
  Pallas kernels  76.3 us (96%)
  local copies, waits for them, and re-layouts  2.17 us (3%)
    pallas_call x1, Pallas kernels, body(): pl.pallas_call(functools.partial(kernel, sizes), out_shape=(jax.ShapeDtyp...  76.3 us
    unnamed x4, local copies, waits for them, and re-layouts  2.17 us

profile of v1, /device:TPU:1, one launch (start us, length us, event | category | flops | bytes accessed | tf_op | source)
XLA Modules:
  0.0 79.1 jit_solution(13316552465802377651)
XLA Ops:
  0.6 76.3 %shard_map.59 = (f32[8,4096]{1,0:T(8,128)}, f32[8,48]{1,0:T(8,128)}) custom-call(bf16[48,4096]{1,0:T(8,128)(2,1)} %k_ref.1, f32[8,48]{1,0:T(8,128)} %obs_ref.1, f32[8,4096]{1,0:T(8,128)} %init_ref.1, f32[8,2,16]{2,1,0:T(2,128)} %bitcast.1), custom_call_target="tpu_custom_call" | custom-call | tf_op jit(solution)/shard_map/pallas_call | solution.py:331
  76.9 0.0 copy-start
  76.9 1.6 %copy.8 = f32[8,4096]{1,0:T(8,128)} copy(f32[8,4096]{1,0:T(8,128)} %get-tuple-element.4) | data formatting | bytes 262144
  78.5 0.0 copy-done
  78.5 0.6 copy.9
Async XLA Ops:
  76.9 1.6 %copy-start = (f32[8,48]{1,0:T(8,128)S(1)}, f32[8,48]{1,0:T(8,128)}, u32[]{:S(2)}) copy-start(f32[8,48]{1,0:T(8,128)} %get-tuple-element.5) | copy-start | bytes 4612

commit v2 on v1

v2 whole, which is shorter than its diff:
```python
import functools

import jax
import jax.numpy as jnp
from jax import lax
from jax.experimental import pallas as pl
from jax.experimental.pallas import tpu as pltpu
from jax.sharding import PartitionSpec as P

MESH = pl.DeviceIdType.MESH
F32 = jnp.float32
BF16 = jnp.bfloat16
LANES = 128
LAYERS = 16
SLOTS = 8

NC, NY, NZ, NV = 2, 8, 4, 16


def lane_of(rows=8):
    return lax.broadcasted_iota(jnp.int32, (rows, LANES), 1)


def shrink(values, cutoff):
    return jnp.where(
        values > cutoff, values - cutoff, jnp.where(values < -cutoff, values + cutoff, 0.0)
    )


def take_prev(tile, edge):
    return jnp.where(lane_of() == 0, edge, pltpu.roll(tile, 1, 1))


def take_next(tile, edge):
    return jnp.where(lane_of() == LANES - 1, edge, pltpu.roll(tile, LANES - 1, 1))


def inverse_wave(smooth, detail, detail_before, smooth_after, detail_after):
    even = smooth - 0.25 * (take_prev(detail, detail_before) + detail)
    even_after = smooth_after - 0.25 * (detail[:, LANES - 1 :] + detail_after)
    odd = detail + 0.5 * (even + take_next(even, even_after))
    return even, odd


def rows_dot(a, b):
    return lax.dot_general(a, b, (((1,), (1,)), ((), ())), preferred_element_type=F32)


def kernel(
    sizes,
    k_hbm,
    obs_hbm,
    init_hbm,
    thr_hbm,
    coef_ref,
    resid_ref,
    k_ref,
    obs_ref,
    init_ref,
    thr_ref,
    pack,
    packs,
    edge_f32,
    edge,
    edges,
    model,
    pred_pad,
    pred_send,
    preds,
    stage,
    parts,
    sums_send,
    sums,
    chunks,
    finals,
    load_sem,
    send_sem,
    recv_sem,
):
    nc, ny, nz, nv = sizes
    groups = nc * nz
    per = LAYERS // groups
    width = per * 2 * LANES
    rows = k_ref.shape[0]
    dp = lax.axis_index("dp")
    vox = lax.axis_index("vox")
    core = lax.rem(dp, nc)
    y = lax.rem(lax.div(dp, nc), ny)
    z = lax.div(dp, nc * ny)
    g = z * nc + core

    loads = [
        pltpu.make_async_copy(init_hbm, init_ref, load_sem.at[0]),
        pltpu.make_async_copy(k_hbm, k_ref, load_sem.at[1]),
        pltpu.make_async_copy(obs_hbm, obs_ref, load_sem.at[2]),
        pltpu.make_async_copy(thr_hbm, thr_ref, load_sem.at[3]),
    ]
    for load in loads:
        load.start()

    def vox_peer(k):
        return dp, lax.rem(vox + k, nv)

    def group_peer(k):
        other = lax.rem(g + k, groups)
        return (lax.div(other, nc) * ny + y) * nc + lax.rem(other, nc), vox

    def y_peer(k):
        return (z * ny + lax.rem(y + k, ny)) * nc + core, vox

    vox_order = sorted(range(1, nv), key=lambda k: -min(k, nv - k))
    y_order = sorted(range(1, ny), key=lambda k: -min(k, ny - k))

    barrier = pltpu.get_barrier_semaphore()

    def greet(peer, k):
        pl.semaphore_signal(barrier, inc=1, device_id=peer(k), device_id_type=MESH)

    for k in vox_order:
        greet(vox_peer, k)
    for k in y_order:
        greet(y_peer, k)
    for k in range(1, groups):
        greet(group_peer, k)

    def send(src, dst, phase, device):
        pltpu.make_async_remote_copy(
            src_ref=src,
            dst_ref=dst,
            send_sem=send_sem.at[phase],
            recv_sem=recv_sem.at[phase],
            device_id=device,
            device_id_type=MESH,
        ).start()

    def wait(ref, sem, phase):
        pltpu.make_async_copy(ref, ref, sem.at[phase]).wait()

    def turn(tile, by):
        by = by % LANES
        return pltpu.roll(tile, by, 1) if by else tile

    lane = lane_of()
    slot = lax.rem(lane, SLOTS)
    loads[0].wait()
    packed = jnp.zeros((8, LANES), F32)
    for layer in range(LAYERS):
        base = layer * 2 * LANES
        smooth = init_ref[:, base : base + LANES]
        detail = init_ref[:, base + LANES : base + 2 * LANES]
        at = layer * SLOTS
        packed = jnp.where(lane == at, turn(smooth, at), packed)
        packed = jnp.where(lane == at + 1, turn(detail, at + 1), packed)
        packed = jnp.where(lane == at + 4, turn(detail, at + 5), packed)
    pack[...] = packed

    pl.semaphore_wait(barrier, (nv - 1) + (groups - 1) + (ny - 1))

    send(pack, packs.at[0], 0, vox_peer(nv - 1))
    send(pack, packs.at[1], 0, vox_peer(1))

    loads[1].wait()
    pick_slot = lax.broadcasted_iota(jnp.int32, (SLOTS, 2 * LANES), 0)
    column = lax.broadcasted_iota(jnp.int32, (SLOTS, 2 * LANES), 1)
    picked = (
        ((pick_slot == 0) & (column == 0))
        | ((pick_slot == 1) & (column == LANES))
        | ((pick_slot == 2) & (column == 1))
        | ((pick_slot == 3) & (column == LANES - 1))
        | ((pick_slot == 4) & (column == 2 * LANES - 1))
    )
    pick = jnp.where(picked, 1.0, 0.0).astype(BF16)
    edge_f32[...] = jnp.zeros_like(edge_f32)
    pred_pad[...] = jnp.zeros_like(pred_pad)
    for layer in range(LAYERS):
        base = layer * 2 * LANES
        edge_f32[layer * SLOTS : (layer + 1) * SLOTS, 0:rows] = rows_dot(
            pick, k_ref[:, base : base + 2 * LANES]
        )
    edge[...] = edge_f32[...].astype(BF16)
    send(edge, edges.at[0], 1, vox_peer(nv - 1))
    send(edge, edges.at[1], 1, vox_peer(1))

    inner = jnp.zeros((8, LANES), F32)
    for layer in range(LAYERS):
        base = layer * 2 * LANES
        at = layer * SLOTS
        smooth = init_ref[:, base : base + LANES]
        detail = init_ref[:, base + LANES : base + 2 * LANES]
        even = smooth - 0.25 * (turn(detail, 1) + detail)
        odd = detail + 0.5 * (even + turn(even, -1))
        inner = jnp.where(lane == at + 1, turn(even, at), inner)
        inner = jnp.where(lane == at + 4, turn(even, at + 5), inner)
        even = jnp.where(lane == 0, 0.0, even)
        odd = jnp.where((lane == 0) | (lane == LANES - 1), 0.0, odd)
        model[:, base : base + LANES] = even.astype(BF16)
        model[:, base + LANES : base + 2 * LANES] = odd.astype(BF16)
    pred_pad[:, 0:rows] = rows_dot(model[...], k_ref[...])
    pred_inner = pred_pad[...]
    detail_first = turn(packed, -1)

    wait(packs, recv_sem, 0)
    after = packs[0]
    before = packs[1]
    even_first = packed - 0.25 * (turn(before, -4) + detail_first)
    odd_first = packed + 0.5 * (turn(even_first, 1) + inner)
    even_after = turn(after, 4) - 0.25 * (packed + turn(after, 3))
    odd_last = packed + 0.5 * (inner + even_after)
    rim = jnp.where(
        slot == 0,
        even_first,
        jnp.where(slot == 1, odd_first, jnp.where(slot == 4, odd_last, 0.0)),
    )
    padded = pred_inner + jnp.dot(rim.astype(BF16), edge[...], preferred_element_type=F32)

    state = []
    for it in range(2):
        phase = 2 + 4 * it
        shared = padded[0:4] + pltpu.roll(padded[4:8], rows, 1)
        pred_send[it] = shared
        preds[it, vox] = shared
        for k in vox_order:
            send(pred_send.at[it], preds.at[it, vox], phase, vox_peer(k))

        if it == 0:
            loads[2].wait()
            loads[3].wait()
            mine = pl.ds(pl.multiple_of(g * width, width), width)
            back = lax.rem(LANES - g * (per * SLOTS), LANES)
            after = pltpu.roll(after, back, 1)
            before = pltpu.roll(before, back, 1)
            pred_pad[:, 64:80] = thr_ref[:, 0, :]
            pred_pad[:, 96:112] = thr_ref[:, 1, :]
            cutoffs = pltpu.roll(pred_pad[...], lax.rem(LANES - g * per, LANES), 1)
            own = init_ref[:, mine]
            cuts = []
            for i in range(per):
                base = i * 2 * LANES
                at = i * SLOTS
                cuts.append(
                    tuple(
                        jnp.broadcast_to(cutoffs[:, c + i : c + i + 1], (8, LANES))
                        for c in (64, 96)
                    )
                )
                state.append(
                    (
                        own[:, base : base + LANES],
                        own[:, base + LANES : base + 2 * LANES],
                        before[:, at + 4 : at + 5],
                        after[:, at : at + 1],
                        after[:, at + 1 : at + 2],
                    )
                )
            wait(edges, recv_sem, 1)
            place = lax.rem(
                lax.broadcasted_iota(jnp.int32, (LAYERS * SLOTS, LANES), 0), SLOTS
            )
            edge_f32[...] = jnp.where(
                place < 3, edges[0].astype(F32), edges[1].astype(F32)
            )
            beyond = edge_f32[:, 0:rows].astype(BF16)

        wait(preds.at[it, pl.ds(0, nv - 1)], recv_sem, phase)
        total = preds[it, 0]
        for j in range(1, nv):
            total = total + preds[it, j]
        predicted = jnp.concatenate(
            [total[:, 0:rows], pltpu.roll(total, LANES - rows, 1)[:, 0:rows]], axis=0
        )
        residual = obs_ref[...] - predicted
        sent = residual.astype(BF16)

        grad = jnp.dot(sent, k_ref[...], preferred_element_type=F32).astype(BF16)
        edge_grad = rows_dot(sent, beyond).astype(BF16)
        for i in range(groups):
            stage[it, i, :, 0:width] = grad[:, i * width : (i + 1) * width]
            stage[it, i, :, width:] = edge_grad

        def send_part(k, carry):
            other = lax.rem(g + k, groups)
            send(stage.at[it, other], parts.at[it, k - 1], phase + 1, group_peer(k))
            return carry

        lax.fori_loop(1, groups, send_part, 0)
        if it == 1:
            resid_ref[...] = residual
        wait(parts.at[it], recv_sem, phase + 1)
        total = stage[it, g].astype(F32)
        for i in range(groups - 1):
            total = total + parts[it, i].astype(F32)
        total = total.astype(BF16)
        sums_send[it] = total
        sums[it, y] = total
        for k in y_order:
            send(sums_send.at[it], sums.at[it, y], phase + 2, y_peer(k))
        wait(sums.at[it, pl.ds(0, ny - 1)], recv_sem, phase + 2)
        total = sums[it, 0].astype(F32)
        for i in range(1, ny):
            total = total + sums[it, i].astype(F32)
        beside = pltpu.roll(total[:, width:], back, 1)

        for i in range(per):
            base = i * 2 * LANES
            at = i * SLOTS
            even = total[:, base : base + LANES]
            odd = total[:, base + LANES : base + 2 * LANES]
            even_after = beside[:, at : at + 1]
            odd_after = beside[:, at + 1 : at + 2]
            even_after2 = beside[:, at + 2 : at + 3]
            even_before = beside[:, at + 3 : at + 4]
            odd_before = beside[:, at + 4 : at + 5]
            detail = odd - 0.5 * (even + take_next(even, even_after))
            detail_before = odd_before - 0.5 * (even_before + even[:, 0:1])
            smooth = even + 0.25 * (take_prev(detail, detail_before) + detail)
            cut_s, cut_d = cuts[i]
            w_s, w_d, w_db, w_sa, w_da = state[i]
            w_s = shrink(w_s + 0.5 * smooth, cut_s)
            w_d = shrink(w_d + 0.5 * detail, cut_d)
            if it == 0:
                detail_after = odd_after - 0.5 * (even_after + even_after2)
                smooth_after = even_after + 0.25 * (detail[:, LANES - 1 :] + detail_after)
                w_db = shrink(w_db + 0.5 * detail_before, cut_d[:, 0:1])
                w_sa = shrink(w_sa + 0.5 * smooth_after, cut_s[:, 0:1])
                w_da = shrink(w_da + 0.5 * detail_after, cut_d[:, 0:1])
                state[i] = (w_s, w_d, w_db, w_sa, w_da)
                w_s, w_d = inverse_wave(w_s, w_d, w_db, w_sa, w_da)
            target = chunks if it == 0 else finals
            target[g, :, base : base + LANES] = w_s.astype(BF16)
            target[g, :, base + LANES : base + 2 * LANES] = w_d.astype(BF16)

        def send_chunk(k, carry):
            send(target.at[g], target.at[g], phase + 3, group_peer(k))
            return carry

        lax.fori_loop(1, groups, send_chunk, 0)
        wait(target.at[pl.ds(0, groups - 1)], recv_sem, phase + 3)
        if it == 0:
            pred = rows_dot(chunks[0], k_ref[:, 0:width])
            for i in range(1, groups):
                pred = pred + rows_dot(chunks[i], k_ref[:, i * width : (i + 1) * width])
            pred_pad[...] = jnp.zeros_like(pred_pad)
            pred_pad[:, 0:rows] = pred
            padded = pred_pad[...]
        else:
            for i in range(groups):
                coef_ref[:, i * width : (i + 1) * width] = finals[i]

    wait(packs, send_sem, 0)
    wait(edges, send_sem, 1)
    for it in range(2):
        phase = 2 + 4 * it
        target = chunks if it == 0 else finals
        wait(preds.at[it, pl.ds(0, nv - 1)], send_sem, phase)
        wait(parts.at[it], send_sem, phase + 1)
        wait(sums.at[it, pl.ds(0, ny - 1)], send_sem, phase + 2)
        wait(target.at[pl.ds(0, groups - 1)], send_sem, phase + 3)


def body(sizes, kernels, observed, initial, threshold):
    nc, ny, nz, nv = sizes
    groups = nc * nz
    width = (LAYERS // groups) * 2 * LANES
    vmem = pl.BlockSpec(memory_space=pltpu.VMEM)
    hbm = pl.BlockSpec(memory_space=pltpu.HBM)
    wide = width + LANES
    cutoffs = jnp.transpose(threshold, (0, 2, 1))
    held = [
        pltpu.with_memory_space_constraint(array, pltpu.HBM)
        for array in (kernels, observed, initial, cutoffs)
    ]
    coefficients, residual = pl.pallas_call(
        functools.partial(kernel, sizes),
        out_shape=(
            jax.ShapeDtypeStruct(initial.shape, BF16),
            jax.ShapeDtypeStruct(observed.shape, F32),
        ),
        in_specs=[hbm] * 4,
        out_specs=(vmem, vmem),
        scratch_shapes=[
            pltpu.VMEM(kernels.shape, BF16),
            pltpu.VMEM(observed.shape, F32),
            pltpu.VMEM(initial.shape, F32),
            pltpu.VMEM(cutoffs.shape, F32),
            pltpu.VMEM((8, LANES), F32),
            pltpu.VMEM((2, 8, LANES), F32),
            pltpu.VMEM((LAYERS * SLOTS, LANES), F32),
            pltpu.VMEM((LAYERS * SLOTS, LANES), BF16),
            pltpu.VMEM((2, LAYERS * SLOTS, LANES), BF16),
            pltpu.VMEM(initial.shape, BF16),
            pltpu.VMEM((8, LANES), F32),
            pltpu.VMEM((2, 4, LANES), F32),
            pltpu.VMEM((2, nv, 4, LANES), F32),
            pltpu.VMEM((2, groups, 8, wide), BF16),
            pltpu.VMEM((2, groups - 1, 8, wide), BF16),
            pltpu.VMEM((2, 8, wide), BF16),
            pltpu.VMEM((2, ny, 8, wide), BF16),
            pltpu.VMEM((groups, 8, width), BF16),
            pltpu.VMEM((groups, 8, width), BF16),
            pltpu.SemaphoreType.DMA((4,)),
            pltpu.SemaphoreType.DMA((10,)),
            pltpu.SemaphoreType.DMA((10,)),
        ],
        compiler_params=pltpu.CompilerParams(
            collective_id=0, has_side_effects=True, vmem_limit_bytes=8 << 20
        ),
    )(*held)
    return coefficients.astype(F32), residual


def build(mesh, sizes):
    return jax.shard_map(
        functools.partial(body, sizes),
        mesh=mesh,
        in_specs=(P("dp", "vox"), P(None, "dp"), P(None, "vox"), P()),
        out_specs=(P(None, "vox"), P(None, "dp")),
        check_vma=False,
    )


def solution(mesh):
    return build(mesh, (NC, NY, NZ, NV))
```

time: 79.3 us -> 75.9 us (0.957)
  Pallas kernels: 76.3 us -> 73.9 us
  local copies, waits for them, and re-layouts: 2.17 us -> 0.59 us
    pallas_call x1, Pallas kernels: 76.3 us -> 73.9 us  [body(): pl.pallas_call(functools.partial(kernel, sizes), out_shape=(jax.ShapeDtyp...]
    unnamed x4 -> x1, local copies, waits for them, and re-layouts: 2.17 us -> 0.59 us
where the time goes in v2:
time: 75.9 us; the launch traced here: 75.8 us
  Pallas kernels  73.9 us (97%)
    pallas_call x1, Pallas kernels, body(): pl.pallas_call(functools.partial(kernel, sizes), out_shape=(jax.ShapeDtyp...  73.9 us

profile of v2, /device:TPU:1, one launch (start us, length us, event | category | flops | bytes accessed | tf_op | source)
XLA Modules:
  0.0 75.8 jit_solution(9734553021711276051)
XLA Ops:
  0.6 73.9 %shard_map.59 = (bf16[8,4096]{1,0:T(8,128)(2,1)S(1)}, f32[8,48]{1,0:T(8,128)S(1)}) custom-call(bf16[48,4096]{1,0:T(8,128)(2,1)} %k_hbm.1, f32[8,48]{1,0:T(8,128)} %obs_hbm.1, f32[8,4096]{1,0:T(8,128)} %init_hbm.1, f32[8,2,16]{2,1,0:T(2,128)} %bitcast.1), custom_call_target="tpu_custom_call" | custom-call | tf_op jit(solution)/shard_map/pallas_call | solution.py:372
  74.5 0.7 convert_element_type.3
  75.2 0.6 copy.7

commit v3 on v2

--- a/solution.py
+++ b/solution.py
@@ -14,7 +14,7 @@
 LAYERS = 16
 SLOTS = 8
 
-NC, NY, NZ, NV = 2, 8, 4, 16
+NC, NY, NZ, NX, NH = 2, 8, 4, 4, 4
 
 
 def lane_of(rows=8):
@@ -76,8 +76,10 @@
     load_sem,
     send_sem,
     recv_sem,
+    beyond_sem,
 ):
-    nc, ny, nz, nv = sizes
+    nc, ny, nz, nx, nh = sizes
+    nv = nx * nh
     groups = nc * nz
     per = LAYERS // groups
     width = per * 2 * LANES
@@ -98,8 +100,15 @@
     for load in loads:
         load.start()
 
-    def vox_peer(k):
+    x = lax.rem(vox, nx)
+    high = lax.div(vox, nx)
+
+    def curve_peer(k):
         return dp, lax.rem(vox + k, nv)
+
+    def vox_peer(by):
+        dh, dx = by
+        return dp, lax.rem(high + dh, nh) * nx + lax.rem(x + dx, nx)
 
     def group_peer(k):
         other = lax.rem(g + k, groups)
@@ -108,7 +117,11 @@
     def y_peer(k):
         return (z * ny + lax.rem(y + k, ny)) * nc + core, vox
 
-    vox_order = sorted(range(1, nv), key=lambda k: -min(k, nv - k))
+    vox_order = sorted(
+        ((dh, dx) for dh in range(nh) for dx in range(nx) if dh or dx),
+        key=lambda by: -(nz * min(by[0], nh - by[0]) + min(by[1], nx - by[1])),
+    )
+    near = [by for by in vox_order if min(by[0], nh - by[0]) < 2]
     y_order = sorted(range(1, ny), key=lambda k: -min(k, ny - k))
 
     barrier = pltpu.get_barrier_semaphore()
@@ -116,8 +129,8 @@
     def greet(peer, k):
         pl.semaphore_signal(barrier, inc=1, device_id=peer(k), device_id_type=MESH)
 
-    for k in vox_order:
-        greet(vox_peer, k)
+    for by in near:
+        greet(vox_peer, by)
     for k in y_order:
         greet(y_peer, k)
     for k in range(1, groups):
@@ -154,10 +167,13 @@
         packed = jnp.where(lane == at + 4, turn(detail, at + 5), packed)
     pack[...] = packed
 
-    pl.semaphore_wait(barrier, (nv - 1) + (groups - 1) + (ny - 1))
-
-    send(pack, packs.at[0], 0, vox_peer(nv - 1))
-    send(pack, packs.at[1], 0, vox_peer(1))
+    pl.semaphore_wait(barrier, len(near) + (groups - 1) + (ny - 1))
+    pl.semaphore_signal(
+        beyond_sem, inc=1, device_id=vox_peer((nh - 1, 0)), device_id_type=MESH
+    )
+
+    send(pack, packs.at[0], 0, curve_peer(nv - 1))
+    send(pack, packs.at[1], 0, curve_peer(1))
 
     loads[1].wait()
     pick_slot = lax.broadcasted_iota(jnp.int32, (SLOTS, 2 * LANES), 0)
@@ -178,8 +194,8 @@
             pick, k_ref[:, base : base + 2 * LANES]
         )
     edge[...] = edge_f32[...].astype(BF16)
-    send(edge, edges.at[0], 1, vox_peer(nv - 1))
-    send(edge, edges.at[1], 1, vox_peer(1))
+    send(edge, edges.at[0], 1, curve_peer(nv - 1))
+    send(edge, edges.at[1], 1, curve_peer(1))
 
     inner = jnp.zeros((8, LANES), F32)
     for layer in range(LAYERS):
@@ -219,8 +235,10 @@
         shared = padded[0:4] + pltpu.roll(padded[4:8], rows, 1)
         pred_send[it] = shared
         preds[it, vox] = shared
-        for k in vox_order:
-            send(pred_send.at[it], preds.at[it, vox], phase, vox_peer(k))
+        if it == 0:
+            pl.semaphore_wait(beyond_sem, 1)
+        for by in vox_order:
+            send(pred_send.at[it], preds.at[it, vox], phase, vox_peer(by))
 
         if it == 0:
             loads[2].wait()
@@ -358,7 +376,8 @@
 
 
 def body(sizes, kernels, observed, initial, threshold):
-    nc, ny, nz, nv = sizes
+    nc, ny, nz, nx, nh = sizes
+    nv = nx * nh
     groups = nc * nz
     width = (LAYERS // groups) * 2 * LANES
     vmem = pl.BlockSpec(memory_space=pltpu.VMEM)
@@ -400,6 +419,7 @@
             pltpu.SemaphoreType.DMA((4,)),
             pltpu.SemaphoreType.DMA((10,)),
             pltpu.SemaphoreType.DMA((10,)),
+            pltpu.SemaphoreType.REGULAR,
         ],
         compiler_params=pltpu.CompilerParams(
             collective_id=0, has_side_effects=True, vmem_limit_bytes=8 << 20
@@ -419,4 +439,4 @@
 
 
 def solution(mesh):
-    return build(mesh, (NC, NY, NZ, NV))
+    return build(mesh, (NC, NY, NZ, NX, NH))

time: 75.9 us -> 74.9 us (0.987)
  Pallas kernels: 73.9 us -> 72.9 us
    pallas_call x1, Pallas kernels: 73.9 us -> 72.9 us  [body(): pl.pallas_call(functools.partial(kernel, sizes), out_shape=(jax.ShapeDtyp...]
where the time goes in v3:
time: 74.9 us; the launch traced here: 74.8 us
  Pallas kernels  72.9 us (97%)
    pallas_call x1, Pallas kernels, body(): pl.pallas_call(functools.partial(kernel, sizes), out_shape=(jax.ShapeDtyp...  72.9 us

profile of v3, /device:TPU:1, one launch (start us, length us, event | category | flops | bytes accessed | tf_op | source)
XLA Modules:
  0.0 74.8 jit_solution(9097746615467869107)
XLA Ops:
  0.6 72.9 %shard_map.59 = (bf16[8,4096]{1,0:T(8,128)(2,1)S(1)}, f32[8,48]{1,0:T(8,128)S(1)}) custom-call(bf16[48,4096]{1,0:T(8,128)(2,1)} %k_hbm.1, f32[8,48]{1,0:T(8,128)} %obs_hbm.1, f32[8,4096]{1,0:T(8,128)} %init_hbm.1, f32[8,2,16]{2,1,0:T(2,128)} %bitcast.1), custom_call_target="tpu_custom_call" | custom-call | tf_op jit(solution)/shard_map/pallas_call | solution.py:391
  73.5 0.7 convert_element_type.3
  74.2 0.6 copy.7

commit v4 on v3

--- a/solution.py
+++ b/solution.py
@@ -110,9 +110,14 @@
         dh, dx = by
         return dp, lax.rem(high + dh, nh) * nx + lax.rem(x + dx, nx)
 
-    def group_peer(k):
-        other = lax.rem(g + k, groups)
-        return (lax.div(other, nc) * ny + y) * nc + lax.rem(other, nc), vox
+    group_order = []
+    if nz == 4:
+        group_order += [(nz - 1 - z, c) for c in range(nc)]
+        group_order += [(lax.rem(z + 2, nz), c) for c in range(nc)]
+    group_order += [(z + 1 - 2 * lax.rem(z, 2), c) for c in range(nc)]
+    group_order += [(z, c) for c in range(1, nc)]
+    group_order = [(oz, lax.rem(core + c, nc)) for oz, c in group_order]
+    group_order = [(oz * nc + oc, (oz * ny + y) * nc + oc) for oz, oc in group_order]
 
     def y_peer(k):
         return (z * ny + lax.rem(y + k, ny)) * nc + core, vox
@@ -133,8 +138,10 @@
         greet(vox_peer, by)
     for k in y_order:
         greet(y_peer, k)
-    for k in range(1, groups):
-        greet(group_peer, k)
+    for _, other in group_order:
+        pl.semaphore_signal(
+            barrier, inc=1, device_id=(other, vox), device_id_type=MESH
+        )
 
     def send(src, dst, phase, device):
         pltpu.make_async_remote_copy(
@@ -295,12 +302,8 @@
             stage[it, i, :, 0:width] = grad[:, i * width : (i + 1) * width]
             stage[it, i, :, width:] = edge_grad
 
-        def send_part(k, carry):
-            other = lax.rem(g + k, groups)
-            send(stage.at[it, other], parts.at[it, k - 1], phase + 1, group_peer(k))
-            return carry
-
-        lax.fori_loop(1, groups, send_part, 0)
+        for i, (chunk, other) in enumerate(group_order):
+            send(stage.at[it, chunk], parts.at[it, i], phase + 1, (other, vox))
         if it == 1:
             resid_ref[...] = residual
         wait(parts.at[it], recv_sem, phase + 1)
@@ -347,11 +350,8 @@
             target[g, :, base : base + LANES] = w_s.astype(BF16)
             target[g, :, base + LANES : base + 2 * LANES] = w_d.astype(BF16)
 
-        def send_chunk(k, carry):
-            send(target.at[g], target.at[g], phase + 3, group_peer(k))
-            return carry
-
-        lax.fori_loop(1, groups, send_chunk, 0)
+        for _, other in group_order:
+            send(target.at[g], target.at[g], phase + 3, (other, vox))
         wait(target.at[pl.ds(0, groups - 1)], recv_sem, phase + 3)
         if it == 0:
             pred = rows_dot(chunks[0], k_ref[:, 0:width])
@@ -373,6 +373,11 @@
         wait(parts.at[it], send_sem, phase + 1)
         wait(sums.at[it, pl.ds(0, ny - 1)], send_sem, phase + 2)
         wait(target.at[pl.ds(0, groups - 1)], send_sem, phase + 3)
+
+
+def finish(narrow_ref, held_ref, coef_ref, resid_ref):
+    coef_ref[...] = narrow_ref[...].astype(F32)
+    resid_ref[...] = held_ref[...]
 
 
 def body(sizes, kernels, observed, initial, threshold):
@@ -425,7 +430,16 @@
             collective_id=0, has_side_effects=True, vmem_limit_bytes=8 << 20
         ),
     )(*held)
-    return coefficients.astype(F32), residual
+    return pl.pallas_call(
+        finish,
+        out_shape=(
+            jax.ShapeDtypeStruct(initial.shape, F32),
+            jax.ShapeDtypeStruct(observed.shape, F32),
+        ),
+        in_specs=[vmem] * 2,
+        out_specs=(vmem, vmem),
+        compiler_params=pltpu.CompilerParams(vmem_limit_bytes=8 << 20),
+    )(coefficients, residual)
 
 
 def build(mesh, sizes):

time: 74.9 us -> 74.2 us (level)
  no operation moved by 1% of the time
where the time goes in v4:
time: 74.2 us; the launch traced here: 74 us
  Pallas kernels  73.4 us (99%)
    pallas_call x1, Pallas kernels, body(): pl.pallas_call(functools.partial(kernel, sizes), out_shape=(jax.ShapeDtyp...  72.7 us

profile of v4, /device:TPU:1, one launch (start us, length us, event | category | flops | bytes accessed | tf_op | source)
XLA Modules:
  0.0 74.0 jit_solution(579274102373510984)
XLA Ops:
  0.6 72.7 %shard_map.59 = (bf16[8,4096]{1,0:T(8,128)(2,1)S(1)}, f32[8,48]{1,0:T(8,128)S(1)}) custom-call(bf16[48,4096]{1,0:T(8,128)(2,1)} %k_hbm.1, f32[8,48]{1,0:T(8,128)} %obs_hbm.1, f32[8,4096]{1,0:T(8,128)} %init_hbm.1, f32[8,2,16]{2,1,0:T(2,128)} %bitcast.1), custom_call_target="tpu_custom_call" | custom-call | tf_op jit(solution)/shard_map/pallas_call | solution.py:396
  73.3 0.7 shard_map.60

commit v5 on v4

--- a/solution.py
+++ b/solution.py
@@ -134,10 +134,10 @@
     def greet(peer, k):
         pl.semaphore_signal(barrier, inc=1, device_id=peer(k), device_id_type=MESH)
 
+    for k in y_order:
+        greet(y_peer, k)
     for by in near:
         greet(vox_peer, by)
-    for k in y_order:
-        greet(y_peer, k)
     for _, other in group_order:
         pl.semaphore_signal(
             barrier, inc=1, device_id=(other, vox), device_id_type=MESH
@@ -201,8 +201,6 @@
             pick, k_ref[:, base : base + 2 * LANES]
         )
     edge[...] = edge_f32[...].astype(BF16)
-    send(edge, edges.at[0], 1, curve_peer(nv - 1))
-    send(edge, edges.at[1], 1, curve_peer(1))
 
     inner = jnp.zeros((8, LANES), F32)
     for layer in range(LAYERS):
@@ -248,6 +246,8 @@
             send(pred_send.at[it], preds.at[it, vox], phase, vox_peer(by))
 
         if it == 0:
+            send(edge, edges.at[0], 1, curve_peer(nv - 1))
+            send(edge, edges.at[1], 1, curve_peer(1))
             loads[2].wait()
             loads[3].wait()
             mine = pl.ds(pl.multiple_of(g * width, width), width)

time: 74.2 us -> 72.9 us (0.982)
  Pallas kernels: 73.4 us -> 72.1 us
    pallas_call x1, Pallas kernels: 72.7 us -> 71.4 us  [body(): pl.pallas_call(functools.partial(kernel, sizes), out_shape=(jax.ShapeDtyp...]
where the time goes in v5:
time: 72.9 us; the launch traced here: 72.7 us
  Pallas kernels  72.1 us (99%)
    pallas_call x1, Pallas kernels, body(): pl.pallas_call(functools.partial(kernel, sizes), out_shape=(jax.ShapeDtyp...  71.4 us

profile of v5, /device:TPU:1, one launch (start us, length us, event | category | flops | bytes accessed | tf_op | source)
XLA Modules:
  0.0 72.7 jit_solution(4891707668482740943)
XLA Ops:
  0.6 71.4 %shard_map.59 = (bf16[8,4096]{1,0:T(8,128)(2,1)S(1)}, f32[8,48]{1,0:T(8,128)S(1)}) custom-call(bf16[48,4096]{1,0:T(8,128)(2,1)} %k_hbm.1, f32[8,48]{1,0:T(8,128)} %obs_hbm.1, f32[8,4096]{1,0:T(8,128)} %init_hbm.1, f32[8,2,16]{2,1,0:T(2,128)} %bitcast.1), custom_call_target="tpu_custom_call" | custom-call | tf_op jit(solution)/shard_map/pallas_call | solution.py:396
  72.1 0.7 shard_map.60

commit v6 on v5

--- a/solution.py
+++ b/solution.py
@@ -62,6 +62,7 @@
     packs,
     edge_f32,
     edge,
+    edge_half,
     edges,
     model,
     pred_pad,
@@ -201,6 +202,10 @@
             pick, k_ref[:, base : base + 2 * LANES]
         )
     edge[...] = edge_f32[...].astype(BF16)
+    half = LAYERS * SLOTS // 2
+    edge_half[...] = (
+        edge_f32[0:half, :] + pltpu.roll(edge_f32[half:, :], LANES // 2, 1)
+    ).astype(BF16)
 
     inner = jnp.zeros((8, LANES), F32)
     for layer in range(LAYERS):
@@ -246,8 +251,8 @@
             send(pred_send.at[it], preds.at[it, vox], phase, vox_peer(by))
 
         if it == 0:
-            send(edge, edges.at[0], 1, curve_peer(nv - 1))
-            send(edge, edges.at[1], 1, curve_peer(1))
+            send(edge_half, edges.at[0], 1, curve_peer(nv - 1))
+            send(edge_half, edges.at[1], 1, curve_peer(1))
             loads[2].wait()
             loads[3].wait()
             mine = pl.ds(pl.multiple_of(g * width, width), width)
@@ -279,11 +284,13 @@
                 )
             wait(edges, recv_sem, 1)
             place = lax.rem(
-                lax.broadcasted_iota(jnp.int32, (LAYERS * SLOTS, LANES), 0), SLOTS
+                lax.broadcasted_iota(jnp.int32, (half, LANES), 0), SLOTS
             )
-            edge_f32[...] = jnp.where(
+            halves = jnp.where(
                 place < 3, edges[0].astype(F32), edges[1].astype(F32)
             )
+            edge_f32[0:half, :] = halves
+            edge_f32[half:, :] = pltpu.roll(halves, LANES // 2, 1)
             beyond = edge_f32[:, 0:rows].astype(BF16)
 
         wait(preds.at[it, pl.ds(0, nv - 1)], recv_sem, phase)
@@ -410,7 +417,8 @@
             pltpu.VMEM((2, 8, LANES), F32),
             pltpu.VMEM((LAYERS * SLOTS, LANES), F32),
             pltpu.VMEM((LAYERS * SLOTS, LANES), BF16),
-            pltpu.VMEM((2, LAYERS * SLOTS, LANES), BF16),
+            pltpu.VMEM((LAYERS * SLOTS // 2, LANES), BF16),
+            pltpu.VMEM((2, LAYERS * SLOTS // 2, LANES), BF16),
             pltpu.VMEM(initial.shape, BF16),
             pltpu.VMEM((8, LANES), F32),
             pltpu.VMEM((2, 4, LANES), F32),

time: 72.9 us -> 73.1 us (level)
  no operation moved by 1% of the time
where the time goes in v6:
time: 73.1 us; the launch traced here: 72.9 us
  Pallas kernels  72.3 us (99%)
    pallas_call x1, Pallas kernels, body(): pl.pallas_call(functools.partial(kernel, sizes), out_shape=(jax.ShapeDtyp...  71.6 us

profile of v6, /device:TPU:1, one launch (start us, length us, event | category | flops | bytes accessed | tf_op | source)
XLA Modules:
  0.0 72.9 jit_solution(3487841945884172819)
XLA Ops:
  0.6 71.6 %shard_map.59 = (bf16[8,4096]{1,0:T(8,128)(2,1)S(1)}, f32[8,48]{1,0:T(8,128)S(1)}) custom-call(bf16[48,4096]{1,0:T(8,128)(2,1)} %k_hbm.1, f32[8,48]{1,0:T(8,128)} %obs_hbm.1, f32[8,4096]{1,0:T(8,128)} %init_hbm.1, f32[8,2,16]{2,1,0:T(2,128)} %bitcast.1), custom_call_target="tpu_custom_call" | custom-call | tf_op jit(solution)/shard_map/pallas_call | solution.py:403
  72.2 0.7 shard_map.60
